TPU v7x, 32 devices: a whole 2x2x4 slice. The times are simulated.
32 devices in a mesh: dp: 4 (over y, x), vocab: 8 (over z, core).
Axes of the slice: x: 2, y: 2, z: 4, core: 2. Of those that a mesh axis runs over, the one named last changes fastest.
Arguments:
- token_ids: int32 [64, 512], P(('dp', 'vocab')), may hold values from 0 to 30719, as said below
- type_ids: int32 [64, 512], P(('dp', 'vocab')), may hold values from 0 to 1
- lengths: int32 [64], P(('dp', 'vocab')), may hold values from 20 to 512, as said below
- word_table: bfloat16 [30720, 768], P('vocab'), may hold values from -6 to 6
- pos_table: bfloat16 [512, 768], replicated, may hold values from -4 to 4
- token_type_embeddings: bfloat16 [2, 768], replicated, may hold values from -4 to 4
- emb_gain: float32 [768], replicated, may hold values from 0.25 to 1.75
- emb_bias: float32 [768], replicated, may hold values from -3 to 3
- query_weight: bfloat16 [768, 768], replicated, may hold values from -0.21875 to 0.21875
- query_bias: float32 [768], replicated, may hold values from -3 to 3
- key_weight: bfloat16 [768, 768], replicated, may hold values from -0.21875 to 0.21875
- value_weight: bfloat16 [768, 768], replicated, may hold values from -0.21875 to 0.21875
- value_bias: float32 [768], replicated, may hold values from -3 to 3
- out_weight: bfloat16 [768, 768], replicated, may hold values from -0.875 to 0.875
- out_bias: float32 [768], replicated, may hold values from -3 to 3
- attn_gain: float32 [768], replicated, may hold values from 0.25 to 1.75
- attn_bias: float32 [768], replicated, may hold values from -3 to 3
- up_weight: bfloat16 [768, 3072], replicated, may hold values from -0.21875 to 0.21875
- up_bias: float32 [3072], replicated, may hold values from -3 to 3
- down_weight: bfloat16 [3072, 768], replicated, may hold values from -0.109375 to 0.109375
- down_bias: float32 [768], replicated, may hold values from -3 to 3
- final_gain: float32 [768], replicated, may hold values from 0.25 to 1.75
- final_bias: float32 [768], replicated, may hold values from -3 to 3
- cotangent: bfloat16 [64, 512, 768], P(('dp', 'vocab')), may hold values from -6 to 6
Outputs:
- encoded: float32 [64, 512, 768], P(('dp', 'vocab'))
- word_grad: float32 [30720, 768], P('vocab')
- pos_grad: float32 [512, 768], P('vocab')
- type_grad: float32 [2, 768], P(None, 'vocab')
- emb_gain_grad: float32 [768], P('vocab')
- emb_bias_grad: float32 [768], P('vocab')
- query_weight_grad: float32 [768, 768], P('vocab')
- query_bias_grad: float32 [768], P('vocab')
- key_weight_grad: float32 [768, 768], P('vocab')
- value_weight_grad: float32 [768, 768], P('vocab')
- value_bias_grad: float32 [768], P('vocab')
- out_weight_grad: float32 [768, 768], P('vocab')
- out_bias_grad: float32 [768], P('vocab')
- attn_gain_grad: float32 [768], P('vocab')
- attn_bias_grad: float32 [768], P('vocab')
- up_weight_grad: float32 [768, 3072], P('vocab')
- up_bias_grad: float32 [3072], P('vocab')
- down_weight_grad: float32 [3072, 768], P('vocab')
- down_bias_grad: float32 [768], P('vocab')
- final_gain_grad: float32 [768], P('vocab')
- final_bias_grad: float32 [768], P('vocab')
Inputs may be any that keep to these rules, and one draw needn't show every extreme that they name: `token_ids`: among the tokens of one device, at most 256 ids fall into the 3840 rows of word_table that one index of vocab holds; for one such block of rows, the same on every device, exactly 256 do. `lengths`: the tokens at positions from a sequence's length on are padding; some sequence has length 512 and some 20.
All inputs are finite; a program needn't handle non-finite values.
Results may differ from a plain program's by a relative error of at most 0.017.
Values may be sent and summed in bfloat16 or wider, within the bound.
A program may use at most 192 MiB of HBM per device.

v0:
```python
from functools import partial
import jax
import jax.numpy as jnp
from jax import lax
from jax.sharding import PartitionSpec as P

HEADS = 12
HEAD = 64
L = 512
EPSILON = 1e-12


def layer_norm(values, gain, bias):
    center = values - jnp.mean(values, -1, keepdims=True)
    spread = jnp.mean(center * center, -1, keepdims=True)
    return center * lax.rsqrt(spread + EPSILON) * gain + bias


def matmul(left, right):
    return jnp.dot(left, right, preferred_element_type=jnp.float32)


def matmul_tn(left, right):
    return lax.dot_general(
        left, right, (((0,), (0,)), ((), ())), preferred_element_type=jnp.float32
    )


def matmul_nt(left, right):
    return lax.dot_general(
        left, right, (((1,), (1,)), ((), ())), preferred_element_type=jnp.float32
    )


def masked_scores(query, keys, length):
    scores = jnp.einsum("qhd,khd->hqk", query, keys, preferred_element_type=jnp.float32) * HEAD ** (
        -0.5
    )
    visible = jnp.arange(L) < length
    return jnp.where(visible[None, None, :], scores, -1000000000.0)


def attend_forward(block):
    query, keys, values, length = block
    scores = masked_scores(query, keys, length)
    highest = jnp.max(scores, -1, keepdims=True)
    expd = jnp.exp(scores - highest)
    totals = jnp.sum(expd, -1, keepdims=True)
    probs_low = (expd / totals).astype(jnp.bfloat16)
    mixed = jnp.einsum("hqk,khd->qhd", probs_low, values, preferred_element_type=jnp.float32)
    return (mixed.astype(jnp.bfloat16), highest + jnp.log(totals))


def attend_backward(block):
    query, keys, values, grad_mixed, logsum, length = block
    probs = jnp.exp(masked_scores(query, keys, length) - logsum)
    probs_low = probs.astype(jnp.bfloat16)
    grad_values = jnp.einsum(
        "hqk,qhd->khd", probs_low, grad_mixed, preferred_element_type=jnp.float32
    )
    grad_probs = jnp.einsum("qhd,khd->hqk", grad_mixed, values, preferred_element_type=jnp.float32)
    inner = jnp.sum(grad_probs * probs, -1, keepdims=True)
    grad_scores = (probs * (grad_probs - inner)).astype(jnp.bfloat16)
    scale = HEAD ** (-0.5)
    grad_query = (
        jnp.einsum("hqk,khd->qhd", grad_scores, keys, preferred_element_type=jnp.float32) * scale
    )
    grad_keys = (
        jnp.einsum("hqk,qhd->khd", grad_scores, query, preferred_element_type=jnp.float32) * scale
    )
    return (grad_query, grad_keys, grad_values)


def local(
    token_ids,
    type_ids,
    lengths,
    word_table,
    pos_table,
    token_type_embeddings,
    emb_gain,
    emb_bias,
    query_weight,
    query_bias,
    key_weight,
    value_weight,
    value_bias,
    out_weight,
    out_bias,
    attn_gain,
    attn_bias,
    up_weight,
    up_bias,
    down_weight,
    down_bias,
    final_gain,
    final_bias,
    cotangent,
):
    seq_count, seq_len = token_ids.shape
    tokens = seq_count * seq_len
    width = word_table.shape[1]
    rows_local = word_table.shape[0]
    owners = lax.axis_size("vocab")
    capacity = max(2, 2 * tokens // owners)
    flat_ids = token_ids.reshape(tokens)
    owner = flat_ids // rows_local
    member = (owner[:, None] == jnp.arange(owners)[None, :]).astype(jnp.int32)
    earlier = jnp.cumsum(member, 0) - member
    rank = jnp.sum(earlier * member, 1)
    slot = owner * capacity + rank
    requests = (
        jnp.full((owners * capacity,), -1, jnp.int32).at[slot].set(flat_ids - owner * rows_local)
    )
    requests = requests.reshape(owners, capacity)
    asked = lax.all_to_all(requests, "vocab", split_axis=0, concat_axis=0, tiled=True)
    valid = asked >= 0
    found = word_table[jnp.maximum(asked, 0)]
    found = jnp.where(valid[..., None], found, jnp.zeros((), jnp.bfloat16))
    returned = lax.all_to_all(found, "vocab", split_axis=0, concat_axis=0, tiled=True)
    word_rows = returned.reshape(owners * capacity, width)[slot]
    kinds = token_type_embeddings.shape[0]
    selection_matrix = (type_ids[..., None] == jnp.arange(kinds)[None, None, :]).astype(jnp.float32)
    type_rows = jnp.einsum(
        "tcr,rb->tcb",
        selection_matrix,
        token_type_embeddings.astype(jnp.float32),
        precision=lax.Precision.HIGHEST,
    )
    embedded = (
        word_rows.reshape(seq_count, seq_len, width).astype(jnp.float32)
        + pos_table.astype(jnp.float32)[None]
        + type_rows
    )
    normed = layer_norm(embedded, emb_gain, emb_bias).reshape(tokens, width)
    normed_low = normed.astype(jnp.bfloat16)
    query = (matmul(normed_low, query_weight) + query_bias).astype(jnp.bfloat16)
    keys = matmul(normed_low, key_weight).astype(jnp.bfloat16)
    values = (matmul(normed_low, value_weight) + value_bias).astype(jnp.bfloat16)
    split_shape = (seq_count, seq_len, HEADS, HEAD)
    query_split = query.reshape(split_shape)
    keys_split = keys.reshape(split_shape)
    values_split = values.reshape(split_shape)
    mixed, logsum = lax.map(attend_forward, (query_split, keys_split, values_split, lengths))
    mixed_low = mixed.reshape(tokens, width)
    first = normed + matmul(mixed_low, out_weight) + out_bias
    hidden = layer_norm(first, attn_gain, attn_bias)
    hidden_reduced_precision = hidden.astype(jnp.bfloat16)
    upper = matmul(hidden_reduced_precision, up_weight) + up_bias
    active_low = jax.nn.gelu(upper, approximate=False).astype(jnp.bfloat16)
    second = hidden + matmul(active_low, down_weight) + down_bias
    encoded = layer_norm(second, final_gain, final_bias)
    grad_out = cotangent.reshape(tokens, width).astype(jnp.float32)
    _, final_pull = jax.vjp(layer_norm, second, final_gain, final_bias)
    grad_second, grad_final_gain, grad_final_bias = final_pull(grad_out)
    grad_down_bias = jnp.sum(grad_second, 0)
    second_matmul_gradient_reduced = grad_second.astype(jnp.bfloat16)
    grad_down = matmul_tn(active_low, second_matmul_gradient_reduced)
    grad_active = matmul_nt(second_matmul_gradient_reduced, down_weight)
    _, gelu_pull = jax.vjp(partial(jax.nn.gelu, approximate=False), upper)
    (grad_upper,) = gelu_pull(grad_active)
    grad_up_bias = jnp.sum(grad_upper, 0)
    grad_upper_low = grad_upper.astype(jnp.bfloat16)
    grad_up = matmul_tn(hidden_reduced_precision, grad_upper_low)
    grad_hidden = grad_second + matmul_nt(grad_upper_low, up_weight)
    _, attn_pull = jax.vjp(layer_norm, first, attn_gain, attn_bias)
    grad_first, grad_attn_gain, grad_attn_bias = attn_pull(grad_hidden)
    grad_out_bias = jnp.sum(grad_first, 0)
    grad_first_low = grad_first.astype(jnp.bfloat16)
    grad_out_weight = matmul_tn(mixed_low, grad_first_low)
    grad_mixed = matmul_nt(grad_first_low, out_weight).astype(jnp.bfloat16)
    grad_query, grad_keys, grad_values = lax.map(
        attend_backward,
        (query_split, keys_split, values_split, grad_mixed.reshape(split_shape), logsum, lengths),
    )
    grad_query = grad_query.reshape(tokens, width)
    grad_keys = grad_keys.reshape(tokens, width)
    grad_values = grad_values.reshape(tokens, width)
    grad_query_bias = jnp.sum(grad_query, 0)
    grad_value_bias = jnp.sum(grad_values, 0)
    grad_query_low = grad_query.astype(jnp.bfloat16)
    grad_keys_low = grad_keys.astype(jnp.bfloat16)
    grad_values_low = grad_values.astype(jnp.bfloat16)
    grad_query_weight = matmul_tn(normed_low, grad_query_low)
    grad_key_weight = matmul_tn(normed_low, grad_keys_low)
    grad_value_weight = matmul_tn(normed_low, grad_values_low)
    grad_normed = (
        grad_first
        + matmul_nt(grad_query_low, query_weight)
        + matmul_nt(grad_keys_low, key_weight)
        + matmul_nt(grad_values_low, value_weight)
    )
    _, emb_pull = jax.vjp(layer_norm, embedded, emb_gain, emb_bias)
    embedding_output_gradient, grad_emb_gain, grad_emb_bias = emb_pull(
        grad_normed.reshape(seq_count, seq_len, width)
    )
    grad_pos = jnp.sum(embedding_output_gradient, 0)
    token_type_gradient = jnp.einsum(
        "nox,noh->xh", selection_matrix, embedding_output_gradient, precision=lax.Precision.HIGHEST
    )
    outgoing = (
        jnp.zeros((owners * capacity, width), jnp.float32)
        .at[slot]
        .set(embedding_output_gradient.reshape(tokens, width))
    )
    incoming = lax.all_to_all(
        outgoing.reshape(owners, capacity, width).astype(jnp.bfloat16),
        "vocab",
        split_axis=0,
        concat_axis=0,
        tiled=True,
    ).astype(jnp.float32)
    keep_rows = asked >= 0
    incoming = jnp.where(keep_rows[..., None], incoming, 0.0)
    grad_word = (
        jnp.zeros((rows_local, width), jnp.float32)
        .at[jnp.maximum(asked, 0).reshape(-1)]
        .add(incoming.reshape(owners * capacity, width))
    )
    (
        grad_query_weight,
        grad_query_bias,
        grad_key_weight,
        grad_value_weight,
        grad_value_bias,
        grad_out_weight,
        grad_out_bias,
        grad_attn_gain,
        grad_attn_bias,
        grad_emb_gain,
        grad_emb_bias,
        grad_pos,
        token_type_gradient,
        grad_down,
        grad_down_bias,
        grad_up,
        grad_up_bias,
        grad_final_gain,
        grad_final_bias,
    ) = (
        lax.psum_scatter(grad_query_weight, "vocab", scatter_dimension=0, tiled=True),
        lax.psum_scatter(grad_query_bias, "vocab", scatter_dimension=0, tiled=True),
        lax.psum_scatter(grad_key_weight, "vocab", scatter_dimension=0, tiled=True),
        lax.psum_scatter(grad_value_weight, "vocab", scatter_dimension=0, tiled=True),
        lax.psum_scatter(grad_value_bias, "vocab", scatter_dimension=0, tiled=True),
        lax.psum_scatter(grad_out_weight, "vocab", scatter_dimension=0, tiled=True),
        lax.psum_scatter(grad_out_bias, "vocab", scatter_dimension=0, tiled=True),
        lax.psum_scatter(grad_attn_gain, "vocab", scatter_dimension=0, tiled=True),
        lax.psum_scatter(grad_attn_bias, "vocab", scatter_dimension=0, tiled=True),
        lax.psum_scatter(grad_emb_gain, "vocab", scatter_dimension=0, tiled=True),
        lax.psum_scatter(grad_emb_bias, "vocab", scatter_dimension=0, tiled=True),
        lax.psum_scatter(grad_pos, "vocab", scatter_dimension=0, tiled=True),
        lax.psum_scatter(token_type_gradient, "vocab", scatter_dimension=1, tiled=True),
        lax.psum_scatter(grad_down, "vocab", scatter_dimension=0, tiled=True),
        lax.psum_scatter(grad_down_bias, "vocab", scatter_dimension=0, tiled=True),
        lax.psum_scatter(grad_up, "vocab", scatter_dimension=0, tiled=True),
        lax.psum_scatter(grad_up_bias, "vocab", scatter_dimension=0, tiled=True),
        lax.psum_scatter(grad_final_gain, "vocab", scatter_dimension=0, tiled=True),
        lax.psum_scatter(grad_final_bias, "vocab", scatter_dimension=0, tiled=True),
    )
    (
        grad_query_weight,
        grad_query_bias,
        grad_key_weight,
        grad_value_weight,
        grad_value_bias,
        grad_out_weight,
        grad_out_bias,
        grad_attn_gain,
        grad_attn_bias,
        grad_emb_gain,
        grad_emb_bias,
        grad_pos,
        token_type_gradient,
        grad_down,
        grad_down_bias,
        grad_up,
        grad_up_bias,
        grad_final_gain,
        grad_final_bias,
        grad_word,
    ) = (
        lax.psum(grad_query_weight.astype(jnp.bfloat16), "dp").astype(jnp.float32),
        lax.psum(grad_query_bias.astype(jnp.bfloat16), "dp").astype(jnp.float32),
        lax.psum(grad_key_weight.astype(jnp.bfloat16), "dp").astype(jnp.float32),
        lax.psum(grad_value_weight.astype(jnp.bfloat16), "dp").astype(jnp.float32),
        lax.psum(grad_value_bias.astype(jnp.bfloat16), "dp").astype(jnp.float32),
        lax.psum(grad_out_weight.astype(jnp.bfloat16), "dp").astype(jnp.float32),
        lax.psum(grad_out_bias.astype(jnp.bfloat16), "dp").astype(jnp.float32),
        lax.psum(grad_attn_gain.astype(jnp.bfloat16), "dp").astype(jnp.float32),
        lax.psum(grad_attn_bias.astype(jnp.bfloat16), "dp").astype(jnp.float32),
        lax.psum(grad_emb_gain.astype(jnp.bfloat16), "dp").astype(jnp.float32),
        lax.psum(grad_emb_bias.astype(jnp.bfloat16), "dp").astype(jnp.float32),
        lax.psum(grad_pos.astype(jnp.bfloat16), "dp").astype(jnp.float32),
        lax.psum(token_type_gradient.astype(jnp.bfloat16), "dp").astype(jnp.float32),
        lax.psum(grad_down.astype(jnp.bfloat16), "dp").astype(jnp.float32),
        lax.psum(grad_down_bias.astype(jnp.bfloat16), "dp").astype(jnp.float32),
        lax.psum(grad_up.astype(jnp.bfloat16), "dp").astype(jnp.float32),
        lax.psum(grad_up_bias.astype(jnp.bfloat16), "dp").astype(jnp.float32),
        lax.psum(grad_final_gain.astype(jnp.bfloat16), "dp").astype(jnp.float32),
        lax.psum(grad_final_bias.astype(jnp.bfloat16), "dp").astype(jnp.float32),
        lax.psum(grad_word.astype(jnp.bfloat16), "dp").astype(jnp.float32),
    )
    return (
        encoded.reshape(seq_count, seq_len, width),
        grad_word,
        grad_pos,
        token_type_gradient,
        grad_emb_gain,
        grad_emb_bias,
        grad_query_weight,
        grad_query_bias,
        grad_key_weight,
        grad_value_weight,
        grad_value_bias,
        grad_out_weight,
        grad_out_bias,
        grad_attn_gain,
        grad_attn_bias,
        grad_up,
        grad_up_bias,
        grad_down,
        grad_down_bias,
        grad_final_gain,
        grad_final_bias,
    )


def solution(mesh):
    placed = (
        P(("dp", "vocab"), None),
        P(("dp", "vocab"), None),
        P(("dp", "vocab")),
        P("vocab", None),
        P(),
        P(),
        P(),
        P(),
        P(),
        P(),
        P(),
        P(),
        P(),
        P(),
        P(),
        P(),
        P(),
        P(),
        P(),
        P(),
        P(),
        P(),
        P(),
        P(("dp", "vocab"), None, None),
    )
    return jax.shard_map(
        local,
        mesh=mesh,
        in_specs=placed,
        out_specs=(
            P(("dp", "vocab"), None, None),
            P("vocab", None),
            P("vocab", None),
            P(None, "vocab"),
            P("vocab"),
            P("vocab"),
            P("vocab", None),
            P("vocab"),
            P("vocab", None),
            P("vocab", None),
            P("vocab"),
            P("vocab", None),
            P("vocab"),
            P("vocab"),
            P("vocab"),
            P("vocab", None),
            P("vocab"),
            P("vocab", None),
            P("vocab"),
            P("vocab"),
            P("vocab"),
        ),
        check_vma=False,
    )
```

profile of v0, /device:TPU:0, one launch (start us, length us, event | category | flops | bytes accessed | tf_op | source)
XLA Modules:
  0.0 1033.5 jit_solution(1598047318248244611)
XLA Ops:
  13.7 4.3 scatter_custom_fusion
  18.1 11.7 %all_to_all.19 = s32[8,1,256]{2,1,0:T(1,128)S(1)} all-to-all(s32[8,1,256]{2,1,0:T(1,128)S(1)} %bitcast.272), channel_id=1, replica_groups=mesh['dp'=4,'vocab'=8] {'vocab'}, dimensions={0} | all-to-all | bytes 16384 | tf_op jit(solution)/shard_map/all_to_all | solution.py:116
  30.4 13.5 %gather_fusion = bf16[2048,768]{1,0:T(8,128)(2,1)} fusion(bf16[3840,768]{1,0:T(8,128)(2,1)} %param.31, s32[2048]{0:T(1024)S(1)} %broadcast_clamp_fusion), kind=kCustom, calls=%fused_computation | custom fusion | bytes 6299648 | tf_op jit(solution)/shard_map/gather | solution.py:118
  44.5 3.3 broadcast_select_fusion
  47.8 4.6 all-to-all-start.1
  52.8 71.1 %all-to-all-done.1 = bf16[8,256,768]{2,1,0:T(8,128)(2,1)} async-done(((bf16[8,256,768]{2,1,0:T(8,128)(2,1)}), bf16[8,256,768]{2,1,0:T(8,128)(2,1)}, u32[]{:S(2)}, u32[]{:S(2)}) %all-to-all-start.1) | async-done | bytes 3145760 | tf_op jit(solution)/shard_map/all_to_all | solution.py:120
  123.9 7.9 gather_fusion.1
  139.9 2.6 convolution_convert_fusion.1
  144.2 2.4 reshape.386
  146.6 3.1 copy.105
  149.6 2.6 add_convert_fusion.1
  153.9 2.4 reshape.384
  156.3 3.0 copy.103
  159.4 2.5 add_convert_fusion
  163.6 2.3 reshape.385
  167.7 25.7 %while.26 = (s32[]{:T(128)}, bf16[2,512,12,64]{1,3,2,0:T(8,128)(2,1)}, f32[2,12,512,1]{2,1,3,0:T(8,128)}, bf16[2,512,12,64]{1,3,2,0:T(8,128)(2,1)}, s32[2]{0:T(1...) while((s32[]{:T(128)}, ...), condition=%wide.region_9.10_spmd, body=%wide.region_6.9_spmd.sunk | while | flops 843442688 | bytes 47411340 | solution.py:144
  169.2 4.1 fusion.155
  173.2 2.6 fusion.156
  175.9 4.2 fusion.157
  181.9 4.1 fusion.155
  186.0 2.6 fusion.156
  188.6 4.2 fusion.157
  193.4 3.6 copy.106
  201.9 35.5 %multiply_convert_fusion.1 = (bf16[1024,3072]{1,0:T(8,128)(2,1)S(1)}, f32[1024,3072]{1,0:T(8,128)}, f32[1024,3072]{1,0:T(8,128)}) fusion(f32[3072]{0:T(1024)S(1)} %copy-done.74, bf16[768,3072]{1,0:T(8,128)(2,1)S(1)} %bitcast.284, f32[1024,768]{1,0:T(8,128)S(1)} %get-tuple-element.280, f32[768]{0:T(1024)S(1)} %copy-done.48, f32[768]{0:T(1024)S(1)} %copy-done.42, ...), kind=kOutput, calls=%fused_computation.64 | convolution fusion | flops 5043388416 | bytes 39348224 | tf_op jit(solution)/shard_map/dot_general | solution.py:20
  237.5 5.4 fusion.98
  246.1 3.5 fusion.92
  249.6 19.6 %fusion.100 = (f32[3072]{0:T(1024)}, bf16[1024,3072]{1,0:T(8,128)(2,1)}) fusion(f32[1024,3072]{1,0:T(8,128)} %get-tuple-element.265, bf16[3072,768]{1,0:T(8,128)(2,1)} %param.47, f32[1024,768]{1,0:T(8,128)} %get-tuple-element.263, f32[1024]{0:T(1024)S(1)} %negate_multiply_fusion.3, f32[1024,3072]{1,0:T(8,128)} %get-tuple-element.281, f32[3072]{0:T(1024)S(1)} %copy-done.74), kind=kOutput, calls=%fused_computation.197 | convolution fusion | flops 4883739648 | bytes 39350272 | tf_op jit(solution)/shard_map/dot_general | solution.py:30
  269.2 11.6 %multiply_reduce_fusion.1 = (f32[768]{0:T(1024)}, f32[1024]{0:T(1024)S(1)}, f32[768]{0:T(1024)}, f32[1024,768]{1,0:T(8,128)S(1)}) fusion(f32[1024,768]{1,0:T(8,128)} %copy-done.7, f32[1024]{0:T(1024)S(1)} %fusion.81, f32[1024]{0:T(1024)S(1)} %broadcast_multiply_fusion.1, f32[768]{0:T(1024)S(1)} %copy-done.42, bf16[768,3072]{1,0:T(8,128)(2,1)} %param.45, ...), kind=kOutput, calls=%fused_computation.96 | convolution fusion | flops 4839699456 | bytes 20472832 | tf_op jit(solution)/shard_map/dot_general | solution.py:30
  287.1 4.0 reshape.389
  291.1 2.9 copy.110
  294.0 55.2 %while.27 = (s32[]{:T(128)}, f32[2,512,12,64]{1,3,2,0:T(8,128)}, bf16[2,512,12,64]{1,3,2,0:T(8,128)(2,1)}, f32[2,512,12,64]{1,3,2,0:T(8,128)}, bf16[2,512,12,64]...) while((s32[]{:T(128)}, f32[2,512,12,64]{1,3,2,0:T(8,128)}, ...), condition=%wide.region_20.21_spmd, body=%wide.region_18.20_spmd.sunk | while | flops 2061232640 | bytes 186580400 | solution.py:172
  295.5 3.1 fusion.166
  298.6 3.0 bitcast_dynamic-update-slice_fusion.11
  301.6 7.3 multiply_reduce_fusion.9
  309.0 7.2 multiply_convert_fusion.3
  322.8 3.1 fusion.166
  325.9 3.0 bitcast_dynamic-update-slice_fusion.11
  328.9 7.3 multiply_reduce_fusion.9
  336.3 7.2 multiply_convert_fusion.3
  349.1 5.5 fusion.94
  371.4 3.4 reduce_sum.274
  374.9 5.3 fusion.86
  380.3 4.7 fusion.104
  385.1 4.8 fusion.103
  389.9 4.2 fusion.105
  394.2 10.7 %fusion.85 = f32[3072,768]{1,0:T(8,128)} fusion(bf16[1024,3072]{1,0:T(8,128)(2,1)} %copy-done.82, f32[1024,768]{1,0:T(8,128)} %get-tuple-element.263, f32[1024]{0:T(1024)S(1)} %copy-done.58), kind=kOutput, calls=%fused_computation.185 | convolution fusion | flops 4833411072 | bytes 18878464 | tf_op jit(solution)/shard_map/dot_general | solution.py:24
  405.6 11.3 %fusion.60 = f32[768,3072]{1,0:T(8,128)} fusion(bf16[1024,3072]{1,0:T(8,128)(2,1)} %get-tuple-element.288, f32[1024,768]{1,0:T(8,128)} %copy-done.7, f32[768]{0:T(1024)S(1)} %copy-done.49, f32[768]{0:T(1024)S(1)} %copy-done.43, f32[1024]{0:T(1024)S(1)} %copy-done.39, f32[1024]{0:T(1024)S(1)} %copy-done.37), kind=kOutput, calls=%fused_computation.101 | convolution fusion | flops 4835770368 | bytes 18888704 | tf_op jit(solution)/shard_map/dot_general | solution.py:24
  416.9 8.7 scatter_custom_fusion.1
  425.6 4.8 convert_element_type.252
  430.4 4.6 all-to-all-start.2
  435.1 5.3 convolution_bitcast_fusion
  442.1 5.9 reduce-scatter.19.cloned.1.call-done
  449.6 70.5 %reduce-scatter.15.cloned.1.call-done = f32[96,768]{1,0:T(8,128)} async-done(((f32[768,768]{1,0:T(8,128)}), f32[96,768]{1,0:T(8,128)}) %reduce-scatter.15.cloned.1.call-update) | async-done | bytes 294928 | tf_op jit(solution)/shard_map/reduce_scatter | solution.py:243
  521.7 44.2 %reduce-scatter.13.cloned.1.call-done = f32[96,768]{1,0:T(8,128)} async-done(((f32[768,768]{1,0:T(8,128)}), f32[96,768]{1,0:T(8,128)}) %reduce-scatter.13.cloned.1.call-update) | async-done | bytes 294928 | tf_op jit(solution)/shard_map/reduce_scatter | solution.py:241
  567.6 36.2 %reduce-scatter.17.cloned.1.call-done = f32[96,768]{1,0:T(8,128)} async-done(((f32[768,768]{1,0:T(8,128)}), f32[96,768]{1,0:T(8,128)}) %reduce-scatter.17.cloned.1.call-update) | async-done | bytes 294928 | tf_op jit(solution)/shard_map/reduce_scatter | solution.py:244
  605.5 4.6 convert_select_fusion
  610.1 20.6 %scatter_custom_fusion.2 = f32[3840,768]{1,0:T(8,128)} fusion(s32[2048]{0:T(1024)} %bitcast.271, f32[2048,768]{1,0:T(8,128)} %bitcast.250, f32[]{:T(128)} %constant.47.clone.1), kind=kCustom, calls=%fused_computation.79 | custom fusion | flops 1572864 | bytes 11796992 | tf_op jit(solution)/shard_map/scatter-add | solution.py:218
  630.7 7.5 convert_element_type.255
  638.2 66.6 %reduce-scatter.23.cloned.1.call-done = f32[384,768]{1,0:T(8,128)} async-done(((f32[3072,768]{1,0:T(8,128)}), f32[384,768]{1,0:T(8,128)}) %reduce-scatter.23.cloned.1.call-update) | async-done | bytes 1179664 | tf_op jit(solution)/shard_map/reduce_scatter | solution.py:254
  706.9 98.1 %reduce-scatter.21.cloned.1.call-done = f32[96,3072]{1,0:T(8,128)} async-done(((f32[768,3072]{1,0:T(8,128)}), f32[96,3072]{1,0:T(8,128)}) %reduce-scatter.21.cloned.1.call-update) | async-done | bytes 1179664 | tf_op jit(solution)/shard_map/reduce_scatter | solution.py:256
  814.6 26.7 %all-reduce.11 = (bf16[768]{0:T(1024)(128)(2,1)S(1)}, bf16[768]{0:T(1024)(128)(2,1)S(1)}, bf16[768]{0:T(1024)(128)(2,1)S(1)}, bf16[768]{0:T(1024)(128)(2,1)S(1)}...) all-reduce(f32[768]{0:T(1024)S(1)} %get-tuple-element.190, ...), channel_id=4, replica_groups=mesh['dp'=4,'vocab'=8] {'vocab'}, use_global_device_ids=true, to_apply=%region_32.33.clone | all-reduce | flops 10752 | bytes 64512
  843.0 10.2 all-reduce.12
  859.5 147.5 %all-reduce.16.cloned.1.call-done = (bf16[3840,768]{1,0:T(8,128)(2,1)}, bf16[64,768]{1,0:T(8,128)(2,1)}, bf16[96,768]{1,0:T(8,128)(2,1)}, bf16[96,768]{1,0:T(8,1...) async-done(((bf16[3840,768]{1,0:T(8,128)(2,1)}, bf16[64,768]{1,0:T(8,128)(2,1)}, ...) | async-done | bytes 7766032 | tf_op jit(solution)/shard_map/psum | solution.py:302
  1018.5 8.2 convert_element_type.256
  (346 shorter events, 109.3 us)
Async XLA Ops:
  7.2 190.3 %copy-start = (bf16[768,768]{1,0:T(8,128)(2,1)S(1)}, bf16[768,768]{1,0:T(8,128)(2,1)}, u32[]{:S(2)}) copy-start(bf16[768,768]{1,0:T(8,128)(2,1)} %param.41) | copy-start | bytes 3538948
  13.7 39.0 %copy-start.59 = (s32[1024,1]{0,1:T(1,128)}, s32[1024,1]{0,1:T(1,128)S(1)}, u32[]{:S(2)}) copy-start(s32[1024,1]{0,1:T(1,128)S(1)} %compare_select_fusion) | copy-start | bytes 12292
  47.8 4.9 copy-start.33
  47.8 76.1 %all-to-all-start.1 = ((bf16[8,256,768]{2,1,0:T(8,128)(2,1)}), bf16[8,256,768]{2,1,0:T(8,128)(2,1)}, u32[]{:S(2)}, u32[]{:S(2)}) async-start(bf16[8,256,768]{2,1,0:T(8,128)(2,1)} %broadcast_select_fusion), calls=%async_computation.1 | async-start | bytes 6291456 | tf_op jit(solution)/shard_map/all_to_all | solution.py:120
  52.4 388.1 %reduce-scatter.11.cloned.1.call-start = ((), (), s32[]{:S(2)}) async-start(), calls=%async_computation.11 | async-start | bytes 1769472 | tf_op jit(solution)/shard_map/reduce_scatter | solution.py:252
  123.9 7.9 copy-start.61
  123.9 7.9 copy-start.69
  134.0 2.9 copy-start.5
  134.0 2.9 copy-start.40
  136.9 3.0 copy-start.70
  144.2 5.5 copy-start.75
  146.6 3.1 copy-start.29
  146.6 3.1 copy-start.31
  153.9 5.4 copy-start.76
  156.3 3.0 copy-start.30
  156.3 3.0 copy-start.72
  163.6 4.1 copy-start.79
  193.4 4.1 copy-start.2
  193.4 4.1 copy-start.17
  193.4 4.1 copy-start.77
  197.5 3.0 slice-start.2
  197.5 3.4 slice-start.3
  197.5 39.9 %slice-start = ((s8[4718592]{0:T(1024)(128)(4,1)}), s8[4194304]{0:T(1024)(128)(4,1)S(1)}, s32[]{:S(2)}) async-start(s8[4718592]{0:T(1024)(128)(4,1)} %bitcast.281), calls=%async_computation.20 | async-start | bytes 8388608
  199.2 38.2 %copy-start.7 = (f32[1024,768]{1,0:T(8,128)}, f32[1024,768]{1,0:T(8,128)S(1)}, u32[]{:S(2)}) copy-start(f32[1024,768]{1,0:T(8,128)S(1)} %get-tuple-element.280) | copy-start | bytes 9437188
  199.2 2.6 copy-start.74
  199.3 81.5 %copy-start.36 = (f32[1024]{0:T(1024)}, f32[1024]{0:T(1024)S(1)}, u32[]{:S(2)}) copy-start(f32[1024]{0:T(1024)S(1)} %broadcast_multiply_fusion.1) | copy-start | bytes 12292
  201.9 78.9 %copy-start.38 = (f32[1024]{0:T(1024)}, f32[1024]{0:T(1024)S(1)}, u32[]{:S(2)}) copy-start(f32[1024]{0:T(1024)S(1)} %fusion.81) | copy-start | bytes 12292
  201.9 35.5 %slice-start.1 = ((s8[4718592]{0:T(1024)(128)(4,1)}), s8[524288]{0:T(1024)(128)(4,1)S(1)}, s32[]{:S(2)}) async-start(s8[4718592]{0:T(1024)(128)(4,1)} %bitcast.281), calls=%async_computation.21 | async-start | bytes 1048576
  201.9 35.6 %copy-start.78 = (f32[768]{0:T(1024)S(1)}, f32[768]{0:T(1024)}, u32[]{:S(2)}) copy-start(f32[768]{0:T(1024)} %param.48) | copy-start | bytes 9220
  237.4 5.5 copy-start.82
  249.6 19.6 %copy-start.57 = (f32[1024]{0:T(1024)}, f32[1024]{0:T(1024)S(1)}, u32[]{:S(2)}) copy-start(f32[1024]{0:T(1024)S(1)} %negate_multiply_fusion.3) | copy-start | bytes 12292
  269.2 11.6 %copy-start.8 = (f32[1024,768]{1,0:T(8,128)S(1)}, f32[1024,768]{1,0:T(8,128)}, u32[]{:S(2)}) copy-start(f32[1024,768]{1,0:T(8,128)} %copy-done.7) | copy-start | bytes 9437188
  287.1 6.9 copy-start.3
  287.1 6.9 copy-start.35
  287.1 6.9 copy-start.80
  295.5 3.1 copy-start.13
  295.5 3.1 copy-start.18
  298.6 3.0 copy-start.12
  301.6 7.3 copy-start.19
  309.0 7.3 copy-start.23
  322.7 3.1 copy-start.13
  322.8 3.1 copy-start.18
  325.9 3.0 copy-start.12
  328.9 7.3 copy-start.19
  336.3 7.3 copy-start.23
  358.8 3.6 copy-start.26
  374.9 73.1 %reduce-scatter.19.cloned.1.call-start = ((), (), s32[]{:S(2)}) async-start(), calls=%async_computation.15 | async-start | bytes 2654208 | tf_op jit(solution)/shard_map/reduce_scatter | solution.py:246
  380.2 139.9 %reduce-scatter.15.cloned.1.call-start = ((), (), s32[]{:S(2)}) async-start(), calls=%async_computation.13 | async-start | bytes 2654208 | tf_op jit(solution)/shard_map/reduce_scatter | solution.py:243
  385.0 181.0 %reduce-scatter.13.cloned.1.call-start = ((), (), s32[]{:S(2)}) async-start(), calls=%async_computation.12 | async-start | bytes 2654208 | tf_op jit(solution)/shard_map/reduce_scatter | solution.py:241
  389.9 4.4 copy-start.58
  389.9 213.9 %reduce-scatter.17.cloned.1.call-start = ((), (), s32[]{:S(2)}) async-start(), calls=%async_computation.14 | async-start | bytes 2654208 | tf_op jit(solution)/shard_map/reduce_scatter | solution.py:244
  394.2 310.6 %reduce-scatter.23.cloned.1.call-start = ((), (), s32[]{:S(2)}) async-start(), calls=%async_computation.17 | async-start | bytes 10616832 | tf_op jit(solution)/shard_map/reduce_scatter | solution.py:254
  404.9 400.0 %reduce-scatter.21.cloned.1.call-start = ((), (), s32[]{:S(2)}) async-start(), calls=%async_computation.16 | async-start | bytes 10616832 | tf_op jit(solution)/shard_map/reduce_scatter | solution.py:256
  430.4 4.7 copy-start.62
  430.4 175.1 %all-to-all-start.2 = ((bf16[8,256,768]{2,1,0:T(8,128)(2,1)}), bf16[8,256,768]{2,1,0:T(8,128)(2,1)}, u32[]{:S(2)}, u32[]{:S(2)}) async-start(bf16[8,256,768]{2,1,0:T(8,128)(2,1)} %bitcast.248), calls=%async_computation.2 | async-start | bytes 6291456 | tf_op jit(solution)/shard_map/all_to_all | solution.py:206
  435.0 170.5 %copy-start.56 = (pred[8,256]{1,0:T(8,128)(4,1)S(1)}, pred[8,256]{1,0:T(8,128)(4,1)}, u32[]{:S(2)}) copy-start(pred[8,256]{1,0:T(8,128)(4,1)} %copy-done.55) | copy-start | bytes 6148
  435.0 407.1 %reduce-scatter.25.cloned.1.call-start = ((), (), s32[]{:S(2)}) async-start(), calls=%async_computation.18 | async-start | bytes 442368
  440.4 566.6 %all-reduce.16.cloned.1.call-start = ((), (), s32[]{:S(2)}) async-start(), calls=%async_computation.19 | async-start | bytes 15532032 | tf_op jit(solution)/shard_map/psum | solution.py:302
  810.1 4.4 copy-start.63
  810.1 4.4 copy-start.64
  810.1 4.4 copy-start.67
  810.1 4.4 copy-start.68
  1007.0 10.4 %copy-start.34 = (bf16[384,768]{1,0:T(8,128)(2,1)S(1)}, bf16[384,768]{1,0:T(8,128)(2,1)}, u32[]{:S(2)}) copy-start(bf16[384,768]{1,0:T(8,128)(2,1)} %get-tuple-element.257) | copy-start | bytes 1769476
  1018.5 8.2 copy-start.1
  (44 other events, 71.6 us)
Sparse Core Ops, SparseCore 0:
  375.0 33.1 reduce-scatter.10
  410.5 37.4 reduce-scatter.18
  450.3 69.7 reduce-scatter.14
  522.3 43.6 reduce-scatter.12
  568.1 35.6 reduce-scatter.16
  606.0 98.7 reduce-scatter.22
  707.1 97.8 reduce-scatter.20
  807.2 29.2 reduce-scatter.24
  843.6 163.4 all-reduce.15
where the time goes:
time: 1040 us; the launch traced here: 1030 us
  waiting for transfers between devices  540 us (52%)
  matrix products  186 us (18%)
  other arithmetic  137 us (13%)
  local copies, waits for them, and re-layouts  95 us (9%)
  blocking collectives  48.7 us (5%)
  between operations  16.5 us (2%)
    psum x1, waiting for transfers between devices, local(): lax.psum(grad_word.astype(jnp.bfloat16), 'dp').astype(jnp.float32)  148 us
    reduce_scatter x1, waiting for transfers between devices, local(): lax.psum_scatter(grad_up, 'vocab', scatter_dimension=0, tiled=True)  98.1 us
    all_to_all x1, waiting for transfers between devices, local(): lax.all_to_all(found, 'vocab', split_axis=0, concat_axis=0, tiled=True)  71.1 us
    reduce_scatter x1, waiting for transfers between devices, local(): lax.psum_scatter(grad_key_weight, 'vocab', scatter_dimension=0, tiled=True)  70.5 us
    reduce_scatter x1, waiting for transfers between devices, local(): lax.psum_scatter(grad_down, 'vocab', scatter_dimension=0, tiled=True)  66.6 us
    dot_general x6, matrix products, matmul(): return jnp.dot(left, right, preferred_element_type=jnp.float32)  50.3 us
    reduce_scatter x1, waiting for transfers between devices, local(): lax.psum_scatter(grad_query_weight, 'vocab', scatter_dimension=0, tiled=T...  44.2 us
    dot_general x6, matrix products, matmul_tn(): lax.dot_general(left, right, (((0,), (0,)), ((), ())), preferred_element_...  40.9 us
  transfers between devices with their start and end apart: 11, of which 8 were waited for; matrix products, arithmetic and copies ran while one was open for 11% of the time, Pallas kernels for 0%

commit v1 on v0

--- a/solution.py
+++ b/solution.py
@@ -299,7 +299,7 @@
         lax.psum(grad_up_bias.astype(jnp.bfloat16), "dp").astype(jnp.float32),
         lax.psum(grad_final_gain.astype(jnp.bfloat16), "dp").astype(jnp.float32),
         lax.psum(grad_final_bias.astype(jnp.bfloat16), "dp").astype(jnp.float32),
-        lax.psum(grad_word.astype(jnp.bfloat16), "dp").astype(jnp.float32),
+        jnp.sum(lax.all_gather(grad_word.astype(jnp.bfloat16), "dp"), axis=0).astype(jnp.float32),
     )
     return (
         encoded.reshape(seq_count, seq_len, width),

time: 1040 us -> 1170 us (1.12)
  waiting for transfers between devices: 540 us -> 653 us
    all_gather x0 -> x1, waiting for transfers between devices: none -> 209 us  [local(): lax.all_gather(grad_word.astype(jnp.bfloat16), 'dp')]
    psum x1, waiting for transfers between devices: 148 us -> 17.6 us  [local(): lax.psum(grad_pos.astype(jnp.bfloat16), 'dp').astype(jnp.float32)]
    reduce_scatter x1, waiting for transfers between devices: 70.5 us -> 36.1 us  [local(): lax.psum_scatter(grad_key_weight, 'vocab', scatter_dimension=0, tiled=True)]
    reduce_scatter x1, waiting for transfers between devices: 66.6 us -> 99.2 us  [local(): lax.psum_scatter(grad_down, 'vocab', scatter_dimension=0, tiled=True)]
    reduce_scatter x1, waiting for transfers between devices: 44.2 us -> 71 us  [local(): lax.psum_scatter(grad_query_weight, 'vocab', scatter_dimension=0, tiled=T...]
    reduce_sum x0 -> x1, other arithmetic: none -> 15.9 us  [local(): jnp.sum(lax.all_gather(grad_word.astype(jnp.bfloat16), 'dp'), axis=0)]
  transfers between devices with their start and end apart: 11 -> 12, of which waited for: 8 -> 9; matrix products, arithmetic and copies ran while one was open for 11% -> 11% of each run, Pallas kernels for 0% -> 0%
where the time goes in v1:
time: 1170 us; the launch traced here: 1160 us
  waiting for transfers between devices  653 us (56%)
  matrix products  188 us (16%)
  other arithmetic  147 us (13%)
  local copies, waits for them, and re-layouts  97 us (8%)
  blocking collectives  48.3 us (4%)
  between operations  16.8 us (1%)
    all_gather x1, waiting for transfers between devices, local(): lax.all_gather(grad_word.astype(jnp.bfloat16), 'dp')  209 us
    reduce_scatter x1, waiting for transfers between devices, local(): lax.psum_scatter(grad_down, 'vocab', scatter_dimension=0, tiled=True)  99.2 us
    reduce_scatter x1, waiting for transfers between devices, local(): lax.psum_scatter(grad_up, 'vocab', scatter_dimension=0, tiled=True)  98.6 us
    all_to_all x1, waiting for transfers between devices, local(): lax.all_to_all(found, 'vocab', split_axis=0, concat_axis=0, tiled=True)  71.1 us
    reduce_scatter x1, waiting for transfers between devices, local(): lax.psum_scatter(grad_query_weight, 'vocab', scatter_dimension=0, tiled=T...  71 us
    dot_general x6, matrix products, matmul(): return jnp.dot(left, right, preferred_element_type=jnp.float32)  50.4 us
    reduce_scatter x1, waiting for transfers between devices, local(): lax.psum_scatter(grad_value_weight, 'vocab', scatter_dimension=0, tiled=T...  44.4 us
    dot_general x6, matrix products, matmul_tn(): lax.dot_general(left, right, (((0,), (0,)), ((), ())), preferred_element_...  40.9 us
  transfers between devices with their start and end apart: 12, of which 9 were waited for; matrix products, arithmetic and copies ran while one was open for 11% of the time, Pallas kernels for 0%

profile of v1, /device:TPU:0, one launch (start us, length us, event | category | flops | bytes accessed | tf_op | source)
XLA Modules:
  0.0 1160.7 jit_solution(6130373292369219467)
XLA Ops:
  13.8 4.3 scatter_custom_fusion
  18.1 11.7 %all_to_all.19 = s32[8,1,256]{2,1,0:T(1,128)S(1)} all-to-all(s32[8,1,256]{2,1,0:T(1,128)S(1)} %bitcast.272), channel_id=1, replica_groups=mesh['dp'=4,'vocab'=8] {'vocab'}, dimensions={0} | all-to-all | bytes 16384 | tf_op jit(solution)/shard_map/all_to_all | solution.py:116
  30.4 13.5 %gather_fusion = bf16[2048,768]{1,0:T(8,128)(2,1)} fusion(bf16[3840,768]{1,0:T(8,128)(2,1)} %param.31, s32[2048]{0:T(1024)S(1)} %broadcast_clamp_fusion), kind=kCustom, calls=%fused_computation | custom fusion | bytes 6299648 | tf_op jit(solution)/shard_map/gather | solution.py:118
  44.5 3.3 broadcast_select_fusion
  47.8 4.6 all-to-all-start.1
  52.8 71.1 %all-to-all-done.1 = bf16[8,256,768]{2,1,0:T(8,128)(2,1)} async-done(((bf16[8,256,768]{2,1,0:T(8,128)(2,1)}), bf16[8,256,768]{2,1,0:T(8,128)(2,1)}, u32[]{:S(2)}, u32[]{:S(2)}) %all-to-all-start.1) | async-done | bytes 3145760 | tf_op jit(solution)/shard_map/all_to_all | solution.py:120
  123.9 7.9 gather_fusion.1
  139.8 2.6 add_convert_fusion.1
  146.5 3.1 copy.124
  149.6 2.6 add_convert_fusion
  158.6 2.6 convolution_convert_fusion.1
  163.7 3.9 reshape.386
  167.6 2.9 copy.126
  170.5 25.6 %while.26 = (s32[]{:T(128)}, bf16[2,512,12,64]{1,3,2,0:T(8,128)(2,1)}, f32[2,12,512,1]{2,1,3,0:T(8,128)}, bf16[2,512,12,64]{1,3,2,0:T(8,128)(2,1)}, s32[2]{0:T(1...) while((s32[]{:T(128)}, ...), condition=%wide.region_9.10_spmd, body=%wide.region_6.9_spmd.sunk | while | flops 843442688 | bytes 47411840 | solution.py:144
  171.9 4.1 fusion.155
  176.0 2.6 fusion.156
  179.2 4.1 fusion.157
  184.6 4.1 fusion.155
  188.7 2.6 fusion.156
  191.9 4.2 fusion.157
  196.1 3.6 copy.127
  204.6 35.5 %multiply_convert_fusion.1 = (bf16[1024,3072]{1,0:T(8,128)(2,1)S(1)}, f32[1024,3072]{1,0:T(8,128)}, f32[1024,3072]{1,0:T(8,128)}) fusion(f32[3072]{0:T(1024)S(1)} %copy-done.77, bf16[768,3072]{1,0:T(8,128)(2,1)S(1)} %bitcast.284, f32[1024,768]{1,0:T(8,128)S(1)} %get-tuple-element.296, f32[768]{0:T(1024)S(1)} %copy-done.51, f32[768]{0:T(1024)S(1)} %copy-done.45, ...), kind=kOutput, calls=%fused_computation.64 | convolution fusion | flops 5043388416 | bytes 39348224 | tf_op jit(solution)/shard_map/dot_general | solution.py:20
  240.2 5.4 fusion.98
  248.8 3.5 fusion.92
  252.3 19.7 %fusion.100 = (f32[3072]{0:T(1024)}, bf16[1024,3072]{1,0:T(8,128)(2,1)}) fusion(f32[1024,3072]{1,0:T(8,128)} %get-tuple-element.281, bf16[3072,768]{1,0:T(8,128)(2,1)} %param.47, f32[1024,768]{1,0:T(8,128)} %get-tuple-element.279, f32[1024]{0:T(1024)S(1)} %negate_multiply_fusion.3, f32[1024,3072]{1,0:T(8,128)} %get-tuple-element.297, f32[3072]{0:T(1024)S(1)} %copy-done.77), kind=kOutput, calls=%fused_computation.197 | convolution fusion | flops 4883739648 | bytes 39350272 | tf_op jit(solution)/shard_map/dot_general | solution.py:30
  272.0 11.6 multiply_reduce_fusion.1
  289.9 4.0 reshape.389
  293.9 2.9 copy.131
  296.8 56.0 %while.27 = (s32[]{:T(128)}, f32[2,512,12,64]{1,3,2,0:T(8,128)}, bf16[2,512,12,64]{1,3,2,0:T(8,128)(2,1)}, f32[2,512,12,64]{1,3,2,0:T(8,128)}, bf16[2,512,12,64]...) while((s32[]{:T(128)}, f32[2,512,12,64]{1,3,2,0:T(8,128)}, ...), condition=%wide.region_20.21_spmd, body=%wide.region_18.20_spmd.sunk | while | flops 2061232640 | bytes 161414480 | solution.py:172
  297.1 3.1 fusion.166
  301.5 7.3 multiply_reduce_fusion.9
  308.8 7.4 multiply_convert_fusion.3
  320.8 3.9 bitcast_dynamic-update-slice_fusion.11
  324.8 3.1 fusion.166
  329.2 7.3 multiply_reduce_fusion.9
  336.5 7.4 multiply_convert_fusion.3
  348.5 3.9 bitcast_dynamic-update-slice_fusion.11
  352.8 5.5 fusion.94
  375.2 3.4 reduce_sum.289
  378.8 5.2 fusion.86
  384.1 4.8 fusion.103
  388.9 4.3 fusion.105
  393.3 4.7 fusion.104
  398.1 10.7 fusion.85
  409.5 11.2 fusion.60
  420.8 8.7 scatter_custom_fusion.1
  429.4 4.8 convert_element_type.254
  434.2 4.6 all-to-all-start.2
  438.9 5.3 convolution_bitcast_fusion
  445.8 6.0 reduce-scatter.19.cloned.1.call-done
  453.5 71.0 %reduce-scatter.13.cloned.1.call-done = f32[96,768]{1,0:T(8,128)} async-done(((f32[768,768]{1,0:T(8,128)}), f32[96,768]{1,0:T(8,128)}) %reduce-scatter.13.cloned.1.call-update) | async-done | bytes 294928 | tf_op jit(solution)/shard_map/reduce_scatter | solution.py:241
  526.1 44.4 %reduce-scatter.17.cloned.1.call-done = f32[96,768]{1,0:T(8,128)} async-done(((f32[768,768]{1,0:T(8,128)}), f32[96,768]{1,0:T(8,128)}) %reduce-scatter.17.cloned.1.call-update) | async-done | bytes 294928 | tf_op jit(solution)/shard_map/reduce_scatter | solution.py:244
  572.1 36.1 %reduce-scatter.15.cloned.1.call-done = f32[96,768]{1,0:T(8,128)} async-done(((f32[768,768]{1,0:T(8,128)}), f32[96,768]{1,0:T(8,128)}) %reduce-scatter.15.cloned.1.call-update) | async-done | bytes 294928 | tf_op jit(solution)/shard_map/reduce_scatter | solution.py:243
  609.9 99.2 %reduce-scatter.23.cloned.1.call-done = f32[384,768]{1,0:T(8,128)} async-done(((f32[3072,768]{1,0:T(8,128)}), f32[384,768]{1,0:T(8,128)}) %reduce-scatter.23.cloned.1.call-update) | async-done | bytes 1179664 | tf_op jit(solution)/shard_map/reduce_scatter | solution.py:254
  711.2 98.6 %reduce-scatter.21.cloned.1.call-done = f32[96,3072]{1,0:T(8,128)} async-done(((f32[768,3072]{1,0:T(8,128)}), f32[96,3072]{1,0:T(8,128)}) %reduce-scatter.21.cloned.1.call-update) | async-done | bytes 1179664 | tf_op jit(solution)/shard_map/reduce_scatter | solution.py:256
  812.1 4.7 convert_select_fusion
  816.8 20.3 %scatter_custom_fusion.2 = f32[3840,768]{1,0:T(8,128)} fusion(s32[2048]{0:T(1024)} %bitcast.271, f32[2048,768]{1,0:T(8,128)} %bitcast.250, f32[]{:T(128)} %constant.48.clone.1), kind=kCustom, calls=%fused_computation.79 | custom fusion | flops 1572864 | bytes 11796992 | tf_op jit(solution)/shard_map/scatter-add | solution.py:218
  837.1 7.4 convert_element_type.257
  850.7 26.4 %all-reduce.11 = (bf16[768]{0:T(1024)(128)(2,1)S(1)}, bf16[768]{0:T(1024)(128)(2,1)S(1)}, bf16[768]{0:T(1024)(128)(2,1)S(1)}, bf16[768]{0:T(1024)(128)(2,1)S(1)}...) all-reduce(f32[768]{0:T(1024)S(1)} %get-tuple-element.207, ...), channel_id=5, replica_groups=mesh['dp'=4,'vocab'=8] {'vocab'}, use_global_device_ids=true, to_apply=%region_32.33.clone | all-reduce | flops 10752 | bytes 64512
  878.8 10.1 all-reduce.12
  895.2 17.6 %all-reduce.16.cloned.1.call-done = (bf16[64,768]{1,0:T(8,128)(2,1)}, bf16[96,768]{1,0:T(8,128)(2,1)}, bf16[96,768]{1,0:T(8,128)(2,1)}, bf16[96,768]{1,0:T(8,128...) async-done(((bf16[64,768]{1,0:T(8,128)(2,1)}, bf16[96,768]{1,0:T(8,128)(2,1)}, bf16[96,768]{1,0:T(8,128)(2,1)}, ...) | async-done | bytes 1867792 | tf_op jit(solution)/shard_map/psum | solution.py:294
  920.9 208.6 %all-gather.3.cloned.1.call-done = bf16[15360,768]{1,0:T(8,128)(2,1)} async-done(((bf16[3840,768]{1,0:T(8,128)(2,1)}), bf16[15360,768]{1,0:T(8,128)(2,1)}) %all-gather.3.cloned.1.call-update) | async-done | bytes 23592976 | tf_op jit(solution)/shard_map/all_gather | solution.py:302
  1129.5 15.9 %reduce_sum.288 = bf16[3840,768]{1,0:T(8,128)(2,1)} reduce(bf16[4,3840,768]{2,1,0:T(8,128)(2,1)} %bitcast.247, bf16[]{:T(256)} %constant.47.clone.1), dimensions={0}, to_apply=%region_25.26 | reduce | flops 8847360 | bytes 29491202 | tf_op jit(solution)/shard_map/reduce_sum | solution.py:302
  1145.4 8.2 convert_element_type.258
  (352 shorter events, 109.5 us)
Async XLA Ops:
  7.2 193.0 %copy-start = (bf16[768,768]{1,0:T(8,128)(2,1)S(1)}, bf16[768,768]{1,0:T(8,128)(2,1)}, u32[]{:S(2)}) copy-start(bf16[768,768]{1,0:T(8,128)(2,1)} %param.41) | copy-start | bytes 3538948
  13.7 39.0 %copy-start.62 = (s32[1024,1]{0,1:T(1,128)}, s32[1024,1]{0,1:T(1,128)S(1)}, u32[]{:S(2)}) copy-start(s32[1024,1]{0,1:T(1,128)S(1)} %compare_select_fusion) | copy-start | bytes 12292
  47.8 4.9 copy-start.32
  47.8 76.1 %all-to-all-start.1 = ((bf16[8,256,768]{2,1,0:T(8,128)(2,1)}), bf16[8,256,768]{2,1,0:T(8,128)(2,1)}, u32[]{:S(2)}, u32[]{:S(2)}) async-start(bf16[8,256,768]{2,1,0:T(8,128)(2,1)} %broadcast_select_fusion), calls=%async_computation.1 | async-start | bytes 6291456 | tf_op jit(solution)/shard_map/all_to_all | solution.py:120
  52.3 391.9 %reduce-scatter.11.cloned.1.call-start = ((), (), s32[]{:S(2)}) async-start(), calls=%async_computation.11 | async-start | bytes 1769472 | tf_op jit(solution)/shard_map/reduce_scatter | solution.py:252
  123.9 7.9 copy-start.64
  123.9 7.9 copy-start.72
  134.0 2.9 copy-start.5
  136.9 2.9 copy-start.30
  136.9 2.9 copy-start.78
  144.1 5.5 copy-start.79
  146.5 3.1 copy-start.28
  146.5 3.1 copy-start.73
  163.7 6.7 copy-start.82
  176.0 3.3 copy-start.11
  188.7 3.3 copy-start.11
  196.1 4.1 copy-start.2
  196.1 4.1 copy-start.18
  196.1 4.1 copy-start.80
  200.2 2.9 slice-start.2
  200.2 3.4 slice-start.3
  200.2 39.9 %slice-start = ((s8[4718592]{0:T(1024)(128)(4,1)}), s8[4194304]{0:T(1024)(128)(4,1)S(1)}, s32[]{:S(2)}) async-start(s8[4718592]{0:T(1024)(128)(4,1)} %bitcast.281), calls=%async_computation.21 | async-start | bytes 8388608
  201.9 38.2 %copy-start.7 = (f32[1024,768]{1,0:T(8,128)}, f32[1024,768]{1,0:T(8,128)S(1)}, u32[]{:S(2)}) copy-start(f32[1024,768]{1,0:T(8,128)S(1)} %get-tuple-element.296) | copy-start | bytes 9437188
  202.0 81.6 %copy-start.34 = (f32[1024]{0:T(1024)}, f32[1024]{0:T(1024)S(1)}, u32[]{:S(2)}) copy-start(f32[1024]{0:T(1024)S(1)} %broadcast_multiply_fusion.1) | copy-start | bytes 12292
  204.6 79.0 %copy-start.36 = (f32[1024]{0:T(1024)}, f32[1024]{0:T(1024)S(1)}, u32[]{:S(2)}) copy-start(f32[1024]{0:T(1024)S(1)} %fusion.81) | copy-start | bytes 12292
  204.6 35.5 %slice-start.1 = ((s8[4718592]{0:T(1024)(128)(4,1)}), s8[524288]{0:T(1024)(128)(4,1)S(1)}, s32[]{:S(2)}) async-start(s8[4718592]{0:T(1024)(128)(4,1)} %bitcast.281), calls=%async_computation.22 | async-start | bytes 1048576
  204.6 35.5 %copy-start.81 = (f32[768]{0:T(1024)S(1)}, f32[768]{0:T(1024)}, u32[]{:S(2)}) copy-start(f32[768]{0:T(1024)} %param.48) | copy-start | bytes 9220
  240.1 5.5 copy-start.85
  252.3 19.7 %copy-start.60 = (f32[1024]{0:T(1024)}, f32[1024]{0:T(1024)S(1)}, u32[]{:S(2)}) copy-start(f32[1024]{0:T(1024)S(1)} %negate_multiply_fusion.3) | copy-start | bytes 12292
  272.0 11.6 copy-start.8
  289.9 6.9 copy-start.3
  289.9 6.9 copy-start.33
  289.9 6.9 copy-start.83
  297.1 4.4 copy-start.12
  297.1 4.4 copy-start.13
  308.8 7.4 copy-start.4
  308.8 7.4 copy-start.19
  324.8 4.4 copy-start.12
  324.8 4.4 copy-start.13
  336.5 7.4 copy-start.4
  336.5 7.4 copy-start.19
  378.7 73.1 %reduce-scatter.19.cloned.1.call-start = ((), (), s32[]{:S(2)}) async-start(), calls=%async_computation.15 | async-start | bytes 2654208 | tf_op jit(solution)/shard_map/reduce_scatter | solution.py:246
  384.0 140.4 %reduce-scatter.13.cloned.1.call-start = ((), (), s32[]{:S(2)}) async-start(), calls=%async_computation.12 | async-start | bytes 2654208 | tf_op jit(solution)/shard_map/reduce_scatter | solution.py:241
  388.9 181.6 %reduce-scatter.17.cloned.1.call-start = ((), (), s32[]{:S(2)}) async-start(), calls=%async_computation.14 | async-start | bytes 2654208 | tf_op jit(solution)/shard_map/reduce_scatter | solution.py:244
  393.3 4.9 copy-start.61
  393.3 214.9 %reduce-scatter.15.cloned.1.call-start = ((), (), s32[]{:S(2)}) async-start(), calls=%async_computation.13 | async-start | bytes 2654208 | tf_op jit(solution)/shard_map/reduce_scatter | solution.py:243
  398.1 311.0 %reduce-scatter.23.cloned.1.call-start = ((), (), s32[]{:S(2)}) async-start(), calls=%async_computation.17 | async-start | bytes 10616832 | tf_op jit(solution)/shard_map/reduce_scatter | solution.py:254
  408.8 401.0 %reduce-scatter.21.cloned.1.call-start = ((), (), s32[]{:S(2)}) async-start(), calls=%async_computation.16 | async-start | bytes 10616832 | tf_op jit(solution)/shard_map/reduce_scatter | solution.py:256
  434.2 4.7 copy-start.65
  434.2 377.9 %all-to-all-start.2 = ((bf16[8,256,768]{2,1,0:T(8,128)(2,1)}), bf16[8,256,768]{2,1,0:T(8,128)(2,1)}, u32[]{:S(2)}, u32[]{:S(2)}) async-start(bf16[8,256,768]{2,1,0:T(8,128)(2,1)} %bitcast.248), calls=%async_computation.2 | async-start | bytes 6291456 | tf_op jit(solution)/shard_map/all_to_all | solution.py:206
  438.8 439.1 %reduce-scatter.25.cloned.1.call-start = ((), (), s32[]{:S(2)}) async-start(), calls=%async_computation.19 | async-start | bytes 442368
  444.2 468.6 %all-reduce.16.cloned.1.call-start = ((), (), s32[]{:S(2)}) async-start(), calls=%async_computation.20 | async-start | bytes 3735552 | tf_op jit(solution)/shard_map/psum | solution.py:294
  526.1 286.0 %copy-start.59 = (pred[8,256]{1,0:T(8,128)(4,1)S(1)}, pred[8,256]{1,0:T(8,128)(4,1)}, u32[]{:S(2)}) copy-start(pred[8,256]{1,0:T(8,128)(4,1)} %copy-done.58) | copy-start | bytes 6148
  812.0 317.4 %all-gather.3.cloned.1.call-start = ((), (), s32[]{:S(2)}) async-start(), calls=%async_computation.18 | async-start | bytes 29491200 | tf_op jit(solution)/shard_map/all_gather | solution.py:302
  847.5 3.1 copy-start.66
  847.5 3.1 copy-start.67
  847.5 3.1 copy-start.70
  847.5 3.1 copy-start.71
  912.8 4.4 copy-start.41
  912.8 5.1 copy-start.40
  912.8 5.9 copy-start.39
  912.8 6.6 copy-start.38
  912.8 7.4 copy-start.44
  1145.4 8.2 copy-start.1
  (46 other events, 77.4 us)
Sparse Core Ops, SparseCore 0:
  378.8 33.1 reduce-scatter.10
  414.3 37.4 reduce-scatter.18
  454.1 70.2 reduce-scatter.12
  526.6 43.8 reduce-scatter.16
  572.7 35.5 reduce-scatter.14
  610.4 98.6 reduce-scatter.22
  712.0 97.8 reduce-scatter.20
  812.1 28.9 reduce-scatter.24
  847.3 65.4 all-reduce.15
  914.7 214.7 all-gather.2
